TPU v7x, 256 devices: a whole 4x4x8 slice. The times are simulated.
256 devices in a mesh: context: 32 (over y, z), head: 2 (over core), dp: 4 (over x).
Axes of the slice: x: 4, y: 4, z: 8, core: 2. Of those that a mesh axis runs over, the one named last changes fastest.
Arguments:
- lin_query: float32 [16384, 4096], P(('dp', 'context'), 'head'), parts along dimension 0, may hold values from -6 to 6
- lin_key: float32 [16384, 4096], P(('dp', 'context'), 'head'), parts along dimension 0, may hold values from -6 to 6
- lin_value: float32 [16384, 4096], P(('dp', 'context'), 'head'), parts along dimension 0, may hold values from -6 to 6
- lin_gate: float32 [16384, 4096], P(('dp', 'context'), 'head'), parts along dimension 0, may hold values from -8 to 8
- decay_rate: float32 [32, 16384], P('head', ('dp', 'context')), parts along dimension 1, may hold values from 0 to 1.5, as said below
- norm_gain: float32 [4096], P('head'), may hold values from 0.5 to 1.5
- sm_query: float32 [16384, 4096], P(('dp', 'context'), 'head'), parts along dimension 0, may hold values from -24 to 24
- sm_key: float32 [16384, 512], P(('dp', 'context'), 'head'), parts along dimension 0, may hold values from -24 to 24
- sm_value: float32 [16384, 512], P(('dp', 'context'), 'head'), parts along dimension 0, may hold values from -6 to 6
- doc_lengths: int32 [64], P('dp'), parts along dimension 0, may hold values from 1 to 3072, 4096 in all
Outputs:
- lin_out: float32 [16384, 4096], P(('dp', 'context'), 'head'), parts along dimension 0
- sm_out: float32 [16384, 4096], P(('dp', 'context'), 'head'), parts along dimension 0
There are 4 independent parts, one for each index of `dp`. A program takes and returns all parts, laid end to end along the dimension named above; an argument that names none is the same for every part. Nothing has to cross between parts.
Inputs may be any that keep to these rules, and one draw needn't show every extreme that they name: `doc_lengths`: the 16 lengths sum to 4096 and the longest is exactly 3072. `decay_rate`: positive rates.
All inputs are finite; a program needn't handle non-finite values.
Results may differ from a plain program's by a relative error of at most 0.0003.
Values sent between devices are 32-bit elements; how exact they have to be, the bound alone decides.
No kernel may reach another device: no remote copies, remote signals or barrier semaphores. Data moves between devices by JAX's collectives and lax.ppermute only.
A program may use at most 192 MiB of HBM per device.

v0:
```python
import jax
import jax.numpy as jnp
from jax import lax
from jax.sharding import PartitionSpec as P

HEAD_DIM = 128
ROT_DIM = 64
rope_base = 10000000.0
norm_eps = 1e-05
highest = lax.Precision.HIGHEST


def entering(value, axis, join, neutral):
    count, mine = (lax.axis_size(axis), lax.axis_index(axis))
    pieces = jax.tree.map(lambda part: lax.all_gather(part, axis), value)
    subtotal = jax.tree.map(
        lambda part, zero: jnp.full_like(part, 0) + jnp.asarray(zero, part.dtype), value, neutral
    )

    def turn(position, subtotal):
        longer = join(subtotal, jax.tree.map(lambda part: part[position], pieces))
        return jax.tree.map(lambda new, old: jnp.where(position < mine, new, old), longer, subtotal)

    return lax.fori_loop(0, count - 1, turn, subtotal)


def doc_tables(doc_lengths):
    doc_ends = jnp.cumsum(doc_lengths)
    doc_starts = doc_ends - doc_lengths
    return (doc_starts, doc_ends)


def doc_number(tokens_at, doc_ends):
    return jnp.sum((doc_ends[None, :] <= tokens_at[:, None]).astype(jnp.int32), axis=1)


def doc_begin(tokens_at, doc_starts):
    picked = jnp.where(doc_starts[None, :] <= tokens_at[:, None], doc_starts[None, :], 0)
    return jnp.max(picked, axis=1)


def lightning_block(
    query_heads, key_heads, value_heads, forgetting_factors, first_token, doc_starts, doc_ends
):
    width = query_heads.shape[1]
    tokens_at = first_token + jnp.arange(width, dtype=jnp.int32)
    doc_ids = doc_number(tokens_at, doc_ends)
    begins = doc_begin(tokens_at, doc_starts)
    log_decay = jnp.cumsum(-forgetting_factors, axis=1)
    visible = (doc_ids[:, None] == doc_ids[None, :]) & (tokens_at[:, None] >= tokens_at[None, :])
    spread = jnp.where(visible[None], log_decay[:, :, None] - log_decay[:, None, :], 0.0)
    weight = jnp.where(visible[None], jnp.exp(spread), 0.0)
    scores = jnp.einsum("htd,hsd->hts", query_heads, key_heads, precision=highest) * weight
    intra = jnp.einsum("hts,hsd->htd", scores, value_heads, precision=highest)
    carried_rows = begins < first_token
    block_decay = jnp.where(carried_rows[-1], jnp.exp(log_decay[:, -1]), 0.0)
    in_tail = doc_ids == doc_ids[-1]
    tail_gap = jnp.where(in_tail[None], log_decay[:, -1:] - log_decay, 0.0)
    tail_weight = jnp.where(in_tail[None], jnp.exp(tail_gap), 0.0)
    block_inner = jnp.einsum(
        "htd,hte->hde", key_heads * tail_weight[:, :, None], value_heads, precision=highest
    )
    return (intra, log_decay, carried_rows, block_decay, block_inner)


def carried_term(query_heads, state, log_decay, carried_rows):
    reach_weight = jnp.where(carried_rows[None], jnp.exp(log_decay), 0.0)
    return (
        jnp.einsum("htd,hde->hte", query_heads, state, precision=highest) * reach_weight[:, :, None]
    )


def finish(attention, lin_gate, norm_gain):
    rows_count = attention.shape[0]
    per_head = attention.reshape(rows_count, -1, HEAD_DIM)
    mean_square = jnp.mean(per_head * per_head, axis=-1, keepdims=True)
    normed = (per_head / jnp.sqrt(mean_square + norm_eps)).reshape(rows_count, -1)
    return normed * norm_gain[None, :] * jax.nn.sigmoid(lin_gate)


def rotate(heads_in, positions):
    half = ROT_DIM // 2
    inverse = rope_base ** (-(2.0 * jnp.arange(half, dtype=jnp.float32)) / ROT_DIM)
    angle = positions.astype(jnp.float32)[:, None] * inverse[None, :]
    cosine = jnp.cos(angle)[:, None, :]
    sine = jnp.sin(angle)[:, None, :]
    first_half = heads_in[..., :half]
    second_half = heads_in[..., half:ROT_DIM]
    return jnp.concatenate(
        [
            first_half * cosine - second_half * sine,
            second_half * cosine + first_half * sine,
            heads_in[..., ROT_DIM:],
        ],
        axis=-1,
    )


def combine_states(earlier, later):
    return (earlier[0] * later[0], later[0][:, None, None] * earlier[1] + later[1])


def shards(
    lin_query,
    lin_key,
    lin_value,
    lin_gate,
    decay_rate,
    norm_gain,
    sm_query,
    sm_key,
    sm_value,
    doc_lengths,
):
    rows_here = lin_query.shape[0]
    lin_heads = lin_query.shape[1] // HEAD_DIM
    kv_local = sm_key.shape[1] // HEAD_DIM
    group = lin_heads // kv_local
    first_token = lax.axis_index("context") * rows_here
    doc_starts, doc_ends = doc_tables(doc_lengths)

    def split_heads(matrix):
        return matrix.reshape(rows_here, -1, HEAD_DIM).transpose(1, 0, 2)

    query_heads = split_heads(lin_query)
    intra, log_decay, carried_rows, block_decay, block_inner = lightning_block(
        query_heads,
        split_heads(lin_key),
        split_heads(lin_value),
        decay_rate,
        first_token,
        doc_starts,
        doc_ends,
    )
    identity = (jnp.ones_like(block_decay), jnp.zeros_like(block_inner))
    prior = entering((block_decay, block_inner), "context", combine_states, identity)
    state = prior[1]
    attention = intra + carried_term(query_heads, state, log_decay, carried_rows)
    attention = attention.transpose(1, 0, 2).reshape(rows_here, lin_heads * HEAD_DIM)
    lin_out = finish(attention, lin_gate, norm_gain)
    tokens_at = first_token + jnp.arange(rows_here, dtype=jnp.int32)
    positions = tokens_at - doc_begin(tokens_at, doc_starts)
    row_docs = doc_number(tokens_at, doc_ends)
    first_begin = doc_begin(first_token[None], doc_starts)[0]
    last_token = first_token + rows_here - 1
    queries = rotate(sm_query.reshape(rows_here, lin_heads, HEAD_DIM), positions)
    queries = queries.reshape(rows_here, kv_local, group, HEAD_DIM).transpose(1, 2, 0, 3)
    keys_rot = rotate(sm_key.reshape(rows_here, kv_local, HEAD_DIM), positions).reshape(
        rows_here, kv_local * HEAD_DIM
    )
    stacked = jnp.stack([keys_rot, sm_value])
    scale = HEAD_DIM ** (-0.5)
    start_carry = (
        jnp.full((kv_local, group, rows_here), -1e30, jnp.float32),
        jnp.zeros((kv_local, group, rows_here), jnp.float32),
        jnp.zeros((kv_local, group, rows_here, HEAD_DIM), jnp.float32),
    )
    piece = lax.all_gather(stacked, "context", axis=1, tiled=True)
    start = jnp.int32(0)
    count = piece.shape[1]
    relevant = (start <= last_token) & (start + count - 1 >= first_begin)

    def attend(current):
        top_old, total_old, summed_old = current
        key_index = jnp.arange(count, dtype=jnp.int32)
        key_docs = doc_number(key_index, doc_ends)
        visible = (
            (key_index[None, :] >= 0)
            & (key_docs[None, :] == row_docs[:, None])
            & (key_index[None, :] <= tokens_at[:, None])
        )
        key_rows = piece[0].reshape(count, kv_local, HEAD_DIM)
        value_rows = piece[1].reshape(count, kv_local, HEAD_DIM)
        scores = jnp.einsum("kgqd,nkd->kgqn", queries, key_rows, precision=highest) * scale
        masked = jnp.where(visible[None, None], scores, -jnp.inf)
        top_new = jnp.maximum(top_old, jnp.max(masked, axis=-1))
        weights = jnp.where(visible[None, None], jnp.exp(masked - top_new[..., None]), 0.0)
        total_new = jnp.sum(weights, axis=-1)
        summed_new = jnp.einsum("kgqn,nkd->kgqd", weights, value_rows, precision=highest)
        return (top_new, total_new, summed_new)

    def keep(current):
        return current

    final_carry = lax.cond(relevant, attend, keep, start_carry)
    mixed = final_carry[2] / final_carry[1][..., None]
    sm_out = mixed.transpose(2, 0, 1, 3).reshape(rows_here, lin_heads * HEAD_DIM)
    return (lin_out, sm_out)


def solution(mesh):
    in_specs = (
        P(("dp", "context"), "head"),
        P(("dp", "context"), "head"),
        P(("dp", "context"), "head"),
        P(("dp", "context"), "head"),
        P("head", ("dp", "context")),
        P("head"),
        P(("dp", "context"), "head"),
        P(("dp", "context"), "head"),
        P(("dp", "context"), "head"),
        P("dp"),
    )
    out_specs = (P(("dp", "context"), "head"), P(("dp", "context"), "head"))
    return jax.shard_map(shards, mesh=mesh, in_specs=in_specs, out_specs=out_specs, check_vma=False)
```

profile of v0, /device:TPU:1, one launch (start us, length us, event | category | flops | bytes accessed | tf_op | source)
XLA Modules:
  0.0 413.0 jit_solution(14850499489194038331)
XLA Ops:
  15.2 1.5 copy.111
  18.0 3.4 fusion.15
  27.5 65.1 %all-reduce = f32[512]{0:T(512)S(1)} all-reduce(f32[512]{0:T(512)S(1)} %dynamic-update-slice), channel_id=2, replica_groups=mesh['context'=32,'head'=2,'dp'=4] {'context'}, use_global_device_ids=true, to_apply=%add | all-reduce | flops 512 | bytes 4096
  95.1 2.9 pad_maximum_fusion
  98.1 2.5 convolution_multiply_fusion
  100.6 2.0 convolution_bitcast_fusion.1
  102.6 15.6 %all-gather.5.cloned.1.call-done = f32[2,4096,256]{1,2,0:T(8,128)} async-done(((f32[2,128,256]{1,2,0:T(8,128)}), f32[2,4096,256]{1,2,0:T(8,128)}) %all-gather.5.cloned.1.call-update) | async-done | bytes 8388624 | tf_op jit(solution)/shard_map/all_gather | solution.py:158
  118.3 91.8 %conditional.1 = (f32[2,8,128]{2,1,0:T(8,128)S(1)}, f32[2,8,128,128]{3,2,1,0:T(8,128)S(1)}) conditional(s32[]{:T(128)} %convert_element_type.19, () %tuple.31, (s32[16]{0:T(128)S(1)}, s32[128]{0:T(128)S(1)}, s32[]{:T(128)}, s32[128]{0:T(128)S(1)}, f32[2,4096,256]{1,2,0:T(8,128)}, /*index=5*/f32[2,8,128,128]{3,2,1,0:T(8,128)}) %tuple.67), branch_computations={%region_8.9_spmd, %region_9.13_spmd} | conditional | flops 25872230400 | bytes 130107472 | solution.py:185
  118.9 4.0 fusion.23
  122.9 35.2 %fusion = (f32[2,8,128]{2,1,0:T(8,128)S(1)}, f32[2,8,128,4096]{3,2,1,0:T(8,128)}) fusion(pred[128,4096]{1,0:T(8,128)(4,1)S(1)} %fusion.8, f32[2,8,128,128]{3,2,1,0:T(8,128)} %get-tuple-element.111, f32[4096,2,128,1]{0,2,3,1:T(8,128)S(1)} %bitcast.95), kind=kOutput, calls=%fused_computation.2 | convolution fusion | flops 12910065664 | bytes 39329792 | tf_op jit(solution)/shard_map/cond/branch_1_fun/kgqd,nkd->kgqn/dot_general | solution.py:174
  158.1 35.1 %fusion.1 = f32[2,8,128,128]{3,2,1,0:T(8,128)S(1)} fusion(f32[4096,2,128,1]{0,2,3,1:T(8,128)S(1)} %bitcast.103, f32[2,8,128,4096]{3,2,1,0:T(8,128)} %get-tuple-element.158, f32[2,8,128]{2,1,0:T(8,128)S(1)} %broadcast_maximum_fusion, pred[128,4096]{1,0:T(8,128)(4,1)S(1)} %fusion.8), kind=kOutput, calls=%fused_computation.3 | convolution fusion | flops 12918456320 | bytes 39329792 | tf_op jit(solution)/shard_map/cond/branch_1_fun/kgqn,nkd->kgqd/dot_general | solution.py:179
  193.2 16.5 %fusion.2 = f32[2,8,128]{2,1,0:T(8,128)S(1)} fusion(f32[2,8,128,4096]{3,2,1,0:T(8,128)} %get-tuple-element.158, f32[2,8,128]{2,1,0:T(8,128)S(1)} %broadcast_maximum_fusion, pred[128,4096]{1,0:T(8,128)(4,1)S(1)} %fusion.8), kind=kLoop, calls=%fused_computation.4 | loop fusion | flops 41940992 | bytes 34095104 | tf_op jit(solution)/shard_map/cond/branch_1_fun/reduce_sum | solution.py:178
  212.3 142.5 %all-gather.7.cloned.1.call-done = f32[512,128,128]{2,1,0:T(8,128)} async-done(((f32[16,128,128]{2,1,0:T(8,128)}), f32[512,128,128]{2,1,0:T(8,128)}) %all-gather.7.cloned.1.call-update) | async-done | bytes 33554448 | tf_op jit(solution)/shard_map/all_gather | solution.py:15
  354.9 46.4 %while.14 = (s32[]{:T(128)}, f32[16,128,128]{2,1,0:T(8,128)S(1)}, s32[]{:T(128)}, f32[32,16]{1,0:T(8,128)S(1)}, f32[32,16,128,128]{3,2,1,0:T(8,128)}, /*index=5*/s32[]{:T(128)}, s32[]{:T(128)}) while((s32[]{:T(128)}, f32[16,128,128]{2,1,0:T(8,128)S(1)}, s32[]{:T(128)}, f32[32,16]{1,0:T(8,128)S(1)}, f32[32,16,128,128]{3,2,1,0:T(8,128)}, ...), condition=%wide.region_5.6_spmd.clone, body=%wide.region_4.5_spmd.clone.sunk | while | flops 1048580 | bytes 3146025 | solution.py:24
  356.4 1.5 fusion.35
  359.4 1.5 fusion.35
  360.9 1.5 fusion.35
  363.9 1.5 fusion.35
  365.4 1.5 fusion.35
  366.9 1.5 fusion.35
  368.4 1.5 fusion.35
  371.4 1.5 fusion.35
  372.9 1.5 fusion.35
  375.9 1.5 fusion.35
  377.4 1.5 fusion.35
  380.4 1.5 fusion.35
  381.9 1.5 fusion.35
  383.4 1.5 fusion.35
  384.9 1.5 fusion.35
  387.9 1.5 fusion.35
  401.3 1.9 multiply_reduce_fusion
  403.7 2.5 divide_multiply_fusion
  (103 shorter events, 42.0 us)
Async XLA Ops:
  7.2 90.9 %copy-start = (f32[128,2048]{1,0:T(8,128)S(1)}, f32[128,2048]{1,0:T(8,128)}, u32[]{:S(2)}) copy-start(f32[128,2048]{1,0:T(8,128)} %param.14) | copy-start | bytes 3145732
  7.2 111.1 %all-gather.5.cloned.1.call-start = ((), (), s32[]{:S(2)}) async-start(), calls=%async_computation | async-start | bytes 8650752 | tf_op jit(solution)/shard_map/all_gather | solution.py:158
  12.6 342.3 %all-gather.7.cloned.1.call-start = ((), (), s32[]{:S(2)}) async-start(), calls=%async_computation.1 | async-start | bytes 34603008 | tf_op jit(solution)/shard_map/all_gather | solution.py:15
  16.7 4.8 %copy-start.1 = (f32[128,2048]{0,1:T(8,128)}, f32[128,2048]{0,1:T(8,128)S(1)}, u32[]{:S(2)}) copy-start(f32[128,2048]{0,1:T(8,128)S(1)} %copy.111) | copy-start | bytes 3145732
  118.3 285.4 %copy-start.2 = (f32[2048]{0:T(1024)S(1)}, f32[2048]{0:T(1024)}, u32[]{:S(2)}) copy-start(f32[2048]{0:T(1024)} %param.19) | copy-start | bytes 24580
Sparse Core Ops, SparseCore 0:
  12.7 105.4 all-gather.4
  121.4 233.4 all-gather.6
where the time goes:
time: 415 us; the launch traced here: 413 us
  waiting for transfers between devices  158 us (38%)
  matrix products  80.1 us (19%)
  other arithmetic  74 us (18%)
  blocking collectives  65.1 us (16%)
  local copies, waits for them, and re-layouts  18.7 us (5%)
  between operations  15.6 us (4%)
    all_gather x1, waiting for transfers between devices, entering(): pieces = jax.tree.map(lambda part: lax.all_gather(part, axis), value)  143 us
    unnamed x1, blocking collectives  65.1 us
    select_n x31, other arithmetic, turn(): jnp.where(position < mine, new, old)  45.2 us
    dot_general x1, matrix products, attend(): jnp.einsum('kgqd,nkd->kgqn', queries, key_rows, precision=highest) * scale  35.2 us
    dot_general x1, matrix products, attend(): jnp.einsum('kgqn,nkd->kgqd', weights, value_rows, precision=highest)  35.1 us
    reduce_sum x1, other arithmetic, attend(): total_new = jnp.sum(weights, axis=-1)  16.5 us
    all_gather x1, waiting for transfers between devices, shards(): piece = lax.all_gather(stacked, 'context', axis=1, tiled=True)  15.6 us
  transfers between devices with their start and end apart: 2, of which 2 were waited for; matrix products, arithmetic and copies ran while one was open for 28% of the time, Pallas kernels for 0%

commit v1 on v0

--- a/solution.py
+++ b/solution.py
@@ -2,6 +2,7 @@
 import jax.numpy as jnp
 from jax import lax
 from jax.sharding import PartitionSpec as P
+from jax.lax import all_to_all, axis_size
 
 HEAD_DIM = 128
 ROT_DIM = 64
@@ -155,7 +156,13 @@
         jnp.zeros((kv_local, group, rows_here), jnp.float32),
         jnp.zeros((kv_local, group, rows_here, HEAD_DIM), jnp.float32),
     )
-    piece = lax.all_gather(stacked, "context", axis=1, tiled=True)
+
+    def notes_update(z):
+        parts_out = all_to_all(jnp.stack([z] * axis_size("context"), axis=0), "context", 0, 0)
+        z1 = jnp.concatenate(parts_out, 1)
+        return z1
+
+    piece = notes_update(stacked)
     start = jnp.int32(0)
     count = piece.shape[1]
     relevant = (start <= last_token) & (start + count - 1 >= first_begin)

time: 415 us -> 559 us (1.35)
  the two profiles are of different devices: /device:TPU:1 before, /device:TPU:2 now
where the time goes in v1:
time: 559 us; the launch traced here: 549 us
  blocking collectives  320 us (57%)
  matrix products  83.3 us (15%)
  other arithmetic  75.5 us (14%)
  local copies, waits for them, and re-layouts  40.7 us (7%)
  between operations  15.9 us (3%)
  starting transfers between devices  11.7 us (2%)
    unnamed x1, blocking collectives  320 us
    select_n x31, other arithmetic, turn(): jnp.where(position < mine, new, old)  45.2 us
    dot_general x1, matrix products, attend(): jnp.einsum('kgqn,nkd->kgqd', weights, value_rows, precision=highest)  36.4 us
    dot_general x1, matrix products, attend(): jnp.einsum('kgqd,nkd->kgqn', queries, key_rows, precision=highest) * scale  35 us
    reduce_sum x1, other arithmetic, attend(): total_new = jnp.sum(weights, axis=-1)  15.9 us
    all_to_all x1, starting transfers between devices, notes_update(): all_to_all(jnp.stack([z] * axis_size('context'), axis=0), 'context', 0, 0)  11.6 us
  transfers between devices with their start and end apart: 2, of which 0 were waited for; matrix products, arithmetic and copies ran while one was open for 25% of the time, Pallas kernels for 0%

profile of v1, /device:TPU:2, one launch (start us, length us, event | category | flops | bytes accessed | tf_op | source)
XLA Modules:
  0.0 548.8 jit_solution(16280913986583332509)
XLA Ops:
  12.2 1.5 copy.78
  15.0 3.4 fusion.18
  21.7 4.2 stack.8
  25.9 11.6 %all-to-all-start = ((f32[32,2,128,256]{2,3,1,0:T(8,128)}), f32[32,2,128,256]{2,3,1,0:T(8,128)}, u32[]{:S(2)}, u32[]{:S(2)}) async-start(f32[32,2,128,256]{2,3,1,0:T(8,128)} %stack.8), calls=%async_computation | async-start | bytes 16777216 | tf_op jit(solution)/shard_map/all_to_all | solution.py:161
  42.9 320.2 %all-reduce = f32[512]{0:T(512)S(1)} all-reduce(f32[512]{0:T(512)S(1)} %dynamic-update-slice), channel_id=2, replica_groups=mesh['context'=32,'head'=2,'dp'=4] {'context'}, use_global_device_ids=true, to_apply=%add | all-reduce | flops 512 | bytes 4096
  365.6 2.9 pad_maximum_fusion
  368.6 2.5 convolution_multiply_fusion
  371.1 3.0 convolution_bitcast_fusion.1
  374.1 111.6 %conditional.1 = (f32[2,8,128]{2,1,0:T(8,128)S(1)}, f32[2,8,128,128]{3,2,1,0:T(8,128)}) conditional(s32[]{:T(128)} %convert_element_type.19, () %tuple.31, (s32[16]{0:T(128)S(1)}, s32[128]{0:T(128)S(1)}, s32[128]{0:T(128)S(1)}, s32[128]{0:T(128)S(1)}, f32[2,32,128,256]{2,3,0,1:T(8,128)}, /*index=5*/f32[2,8,128,128]{3,2,1,0:T(8,128)}) %tuple.67), branch_computations={%region_8.9_spmd, %region_9.13_spmd} | conditional | flops 25872230400 | bytes 163662416 | solution.py:192
  375.1 8.4 %copy.67 = f32[2,32,128,256]{2,1,3,0:T(8,128)S(1)} copy(f32[2,32,128,256]{2,3,0,1:T(8,128)} %get-tuple-element.149) | data formatting | bytes 16777216 | tf_op jit(solution)/shard_map
  383.4 4.4 fusion.26
  387.8 5.5 squeeze.20
  393.3 35.0 %fusion = (f32[2,8,128]{2,1,0:T(8,128)S(1)}, f32[2,8,128,4096]{3,2,1,0:T(8,128)}) fusion(pred[128,4096]{1,0:T(8,128)(4,1)S(1)} %fusion.11, f32[2,8,128,128]{3,2,1,0:T(8,128)} %get-tuple-element.111, f32[4096,2,128]{0,2,1:T(8,128)} %squeeze.20), kind=kOutput, calls=%fused_computation.2 | convolution fusion | flops 12910065664 | bytes 39329792 | tf_op jit(solution)/shard_map/cond/branch_1_fun/kgqd,nkd->kgqn/dot_general | solution.py:181
  428.3 4.9 squeeze.21
  433.2 36.4 %fusion.1 = f32[2,8,128,128]{3,2,1,0:T(8,128)} fusion(f32[2,8,128,4096]{3,2,1,0:T(8,128)} %get-tuple-element.170, f32[2,8,128]{2,1,0:T(8,128)S(1)} %broadcast_maximum_fusion, pred[128,4096]{1,0:T(8,128)(4,1)S(1)} %fusion.11, f32[4096,2,128]{0,2,1:T(8,128)} %squeeze.21), kind=kOutput, calls=%fused_computation.3 | convolution fusion | flops 12918456320 | bytes 39329792 | tf_op jit(solution)/shard_map/cond/branch_1_fun/kgqn,nkd->kgqd/dot_general | solution.py:186
  469.6 15.9 %fusion.2 = f32[2,8,128]{2,1,0:T(8,128)S(1)} fusion(f32[2,8,128,4096]{3,2,1,0:T(8,128)} %get-tuple-element.170, f32[2,8,128]{2,1,0:T(8,128)S(1)} %broadcast_maximum_fusion, pred[128,4096]{1,0:T(8,128)(4,1)S(1)} %fusion.11), kind=kLoop, calls=%fused_computation.4 | loop fusion | flops 41940992 | bytes 34095104 | tf_op jit(solution)/shard_map/cond/branch_1_fun/reduce_sum | solution.py:185
  485.7 1.6 divide_bitcast_fusion
  489.2 46.4 %while.14 = (s32[]{:T(128)}, f32[16,128,128]{2,1,0:T(8,128)S(1)}, s32[]{:T(128)}, f32[32,16]{1,0:T(8,128)S(1)}, f32[32,16,128,128]{3,2,1,0:T(8,128)}, /*index=5*/s32[]{:T(128)}, s32[]{:T(128)}) while((s32[]{:T(128)}, f32[16,128,128]{2,1,0:T(8,128)S(1)}, s32[]{:T(128)}, f32[32,16]{1,0:T(8,128)S(1)}, f32[32,16,128,128]{3,2,1,0:T(8,128)}, ...), condition=%wide.region_5.6_spmd.clone, body=%wide.region_4.5_spmd.clone.sunk | while | flops 1048580 | bytes 3146025 | solution.py:25
  492.2 1.5 fusion.36
  493.7 1.5 fusion.36
  496.7 1.5 fusion.36
  498.2 1.5 fusion.36
  499.7 1.5 fusion.36
  501.2 1.5 fusion.36
  504.2 1.5 fusion.36
  505.7 1.5 fusion.36
  508.7 1.5 fusion.36
  510.2 1.5 fusion.36
  511.7 1.5 fusion.36
  513.2 1.5 fusion.36
  535.7 3.1 multiply_reduce_fusion
  539.2 2.5 divide_multiply_fusion
  (108 shorter events, 47.0 us)
Async XLA Ops:
  7.2 361.5 %copy-start = (f32[128,2048]{1,0:T(8,128)S(1)}, f32[128,2048]{1,0:T(8,128)}, u32[]{:S(2)}) copy-start(f32[128,2048]{1,0:T(8,128)} %param.14) | copy-start | bytes 3145732
  7.2 34.2 %copy-start.3 = (u32[256]{0:T(256)S(1)}, u32[256]{0:T(256)}, u32[]{:S(2)}) copy-start(u32[256]{0:T(256)} %constant.80) | copy-start | bytes 3076
  7.2 482.0 %all-gather.4.cloned.1.call-start = ((), (), s32[]{:S(2)}) async-start(), calls=%async_computation.1 | async-start | bytes 34603008 | tf_op jit(solution)/shard_map/all_gather | solution.py:16
  13.7 23.8 %copy-start.1 = (f32[128,2048]{0,1:T(8,128)}, f32[128,2048]{0,1:T(8,128)S(1)}, u32[]{:S(2)}) copy-start(f32[128,2048]{0,1:T(8,128)S(1)} %copy.78) | copy-start | bytes 3145732
  25.9 348.2 %all-to-all-start = ((f32[32,2,128,256]{2,3,1,0:T(8,128)}), f32[32,2,128,256]{2,3,1,0:T(8,128)}, u32[]{:S(2)}, u32[]{:S(2)}) async-start(f32[32,2,128,256]{2,3,1,0:T(8,128)} %stack.8), calls=%async_computation | async-start | bytes 16777216 | tf_op jit(solution)/shard_map/all_to_all | solution.py:161
  374.1 165.1 %copy-start.2 = (f32[2048]{0:T(1024)S(1)}, f32[2048]{0:T(1024)}, u32[]{:S(2)}) copy-start(f32[2048]{0:T(1024)} %param.19) | copy-start | bytes 24580
Sparse Core Ops, SparseCore 0:
  18.5 401.7 all-gather.3
